TPU v7x, 32 devices: a whole 2x2x4 slice. The times are simulated.
32 devices in a mesh: dp: 4 (over y, x), expert: 4 (over z), tok: 2 (over core).
Axes of the slice: x: 2, y: 2, z: 4, core: 2. Of those that a mesh axis runs over, the one named last changes fastest.
Arguments:
- tokens: bfloat16 [32768, 512], P(('dp', 'expert', 'tok')), may hold values from -6 to 6
- out_grad: bfloat16 [32768, 512], P(('dp', 'expert', 'tok')), may hold values from -6 to 6
- expert_ids: int32 [32768, 2], P(('dp', 'expert', 'tok')), may hold values from 0 to 3, all different within a row; in each aligned block of 1024 rows (0 to 1023, 1024 to 2047, ...) at most 768 rows name the same one
- sentence_ids: int32 [32, 1024], P(('dp', 'expert', 'tok')), may hold values from 0 to 15, never falling along the last dimension, each value on 1 to 128 neighbouring positions
- ln_attn: float32 [512], replicated, may hold values from 0.25 to 1.75
- w_kv: bfloat16 [512, 128], replicated, may hold values from -0.25 to 0.25
- w_router: bfloat16 [512, 4], replicated, may hold values from -0.1875 to 0.1875
- w_query: bfloat16 [4, 512, 64], P('expert'), may hold values from -0.25 to 0.25
- w_output: bfloat16 [4, 64, 512], P('expert'), may hold values from -4 to 4
- ln_ffn: float32 [512], replicated, may hold values from 0.25 to 1.75
- w_in: bfloat16 [512, 2048], replicated, may hold values from -0.25 to 0.25
- w_out: bfloat16 [2048, 512], replicated, may hold values from -0.1875 to 0.1875
Outputs:
- output: bfloat16 [32768, 512], P(('dp', 'expert', 'tok'))
- grad_tokens: bfloat16 [32768, 512], P(('dp', 'expert', 'tok'))
- grad_ln_attn: float32 [512], replicated
- grad_kv: float32 [512, 128], replicated
- grad_router: float32 [512, 4], replicated
- grad_query: float32 [4, 512, 64], P('expert')
- grad_output: float32 [4, 64, 512], P('expert')
- grad_ln_ffn: float32 [512], replicated
- grad_in: float32 [512, 2048], replicated
- grad_out: float32 [2048, 512], replicated
Inputs may be any that keep to these rules, and one draw needn't show every extreme that they name: `expert_ids`: among the 1024 rows of one device no expert is named more than 768 times, a bound that some block reaches; a token's 2 ids differ. `sentence_ids`: in each device's row the ids never fall; each id covers 1 to 128 consecutive positions, one exactly 128.
All inputs are finite; a program needn't handle non-finite values.
Results may differ from a plain program's by a relative error of at most 0.017.
Values may be sent and summed in bfloat16 or wider, within the bound.
No kernel may reach another device: no remote copies, remote signals or barrier semaphores. Data moves between devices by JAX's collectives and lax.ppermute only.
A program may use at most 128 MiB of HBM per device.

v0:
```python
import jax
import jax.numpy as jnp
from jax import lax
from jax.sharding import PartitionSpec as P


def product(left, right):
    return jnp.dot(left, right, preferred_element_type=jnp.float32)


def product_tn(left, right):
    return lax.dot_general(
        left, right, (((0,), (0,)), ((), ())), preferred_element_type=jnp.float32
    )


def product_nt(left, right):
    return lax.dot_general(
        left, right, (((1,), (1,)), ((), ())), preferred_element_type=jnp.float32
    )


def layer_norm_parts(values, gain):
    centre = values - jnp.mean(values, axis=-1, keepdims=True)
    spread = jnp.mean(centre * centre, axis=-1, keepdims=True)
    inverse = lax.rsqrt(spread + 1e-05)
    normalized = centre * inverse
    return (normalized * gain, normalized, inverse)


def layer_norm_back(upstream, normalized, inverse, gain):
    scaled = upstream * gain
    gain_grad = jnp.sum(upstream * normalized, axis=0)
    inner = (
        scaled
        - jnp.mean(scaled, axis=-1, keepdims=True)
        - normalized * jnp.mean(scaled * normalized, axis=-1, keepdims=True)
    )
    return (inner * inverse, gain_grad)


def gelu_exact(values):
    return 0.5 * values * (1.0 + jax.scipy.special.erf(values * 0.7071067811865476))


def gelu_slope(values):
    cumulative = 0.5 * (1.0 + jax.scipy.special.erf(values * 0.7071067811865476))
    density = jnp.exp(-0.5 * values * values) * 0.3989422804014327
    return cumulative + values * density


def head_forward(rows, row_ids, shared, key_ids, query_weight, output_weight):
    head_size = query_weight.shape[1]
    queries = product(rows, query_weight).astype(jnp.bfloat16)
    scores = product_nt(queries, shared[:, :head_size]) * 0.125
    scores = jnp.where(row_ids[:, None] == key_ids[None, :], scores, -30000.0)
    largest = jnp.max(scores, axis=-1, keepdims=True)
    raised = jnp.exp(scores - largest)
    total = jnp.sum(raised, axis=-1, keepdims=True)
    weights = (raised / total).astype(jnp.bfloat16)
    attended = product(weights, shared[:, head_size:]).astype(jnp.bfloat16)
    result = product(attended, output_weight).astype(jnp.bfloat16)
    log_total = largest[:, 0] + jnp.log(total[:, 0])
    return (result, queries, attended, log_total)


def head_backward(
    rows,
    row_ids,
    shared,
    key_ids,
    query_weight,
    output_weight,
    queries,
    attended,
    log_total,
    result_grad,
):
    head_size = query_weight.shape[1]
    output_grad = product_tn(attended, result_grad)
    attended_grad = product_nt(result_grad, output_weight).astype(jnp.bfloat16)
    scores = product_nt(queries, shared[:, :head_size]) * 0.125
    scores = jnp.where(row_ids[:, None] == key_ids[None, :], scores, -30000.0)
    probs = jnp.exp(scores - log_total[:, None])
    prob_low = probs.astype(jnp.bfloat16)
    prob_grad = product_nt(attended_grad, shared[:, head_size:])
    score_grad = (probs * (prob_grad - jnp.sum(probs * prob_grad, axis=-1, keepdims=True))).astype(
        jnp.bfloat16
    )
    query_grad = (product(score_grad, shared[:, :head_size]) * 0.125).astype(jnp.bfloat16)
    key_grad = product_tn(score_grad, queries) * 0.125
    value_grad = product_tn(prob_low, attended_grad)
    shared_grad = jnp.concatenate([key_grad, value_grad], axis=1)
    query_weight_grad = product_tn(rows, query_grad)
    rows_grad = product_nt(query_grad, query_weight).astype(jnp.bfloat16)
    return (rows_grad, shared_grad, query_weight_grad, output_grad)


def body(
    tokens,
    out_grad,
    expert_ids,
    sentence_ids,
    ln_attn,
    w_kv,
    w_router,
    w_query,
    w_output,
    ln_ffn,
    w_in,
    w_out,
):
    length = tokens.shape[0]
    width = tokens.shape[1]
    choose = expert_ids.shape[1]
    head_size = w_query.shape[2]
    experts = lax.axis_size("expert")
    capacity = 3 * length // experts
    sentence = sentence_ids[0]
    inputs = tokens.astype(jnp.float32)
    normed, norm_one, inverse_one = layer_norm_parts(inputs, ln_attn)
    normed_low = normed.astype(jnp.bfloat16)
    shared = product(normed_low, w_kv).astype(jnp.bfloat16)
    logits = product(normed_low, w_router)
    expert_range = jnp.arange(experts, dtype=jnp.int32)
    selector = (expert_ids[:, :, None] == expert_range[None, None, :]).astype(jnp.float32)
    picked = jnp.sum(selector * logits[:, None, :], axis=2)
    picked_top = jnp.max(picked, axis=-1, keepdims=True)
    picked_raised = jnp.exp(picked - picked_top)
    gates = picked_raised / jnp.sum(picked_raised, axis=-1, keepdims=True)
    flat_expert = expert_ids.reshape(length * choose)
    member = (flat_expert[:, None] == expert_range[None, :]).astype(jnp.int32)
    earlier = jnp.cumsum(member, axis=0) - member
    position = jnp.sum(earlier * member, axis=1)
    slot_index = flat_expert * capacity + position
    routed_rows = jnp.broadcast_to(normed_low[:, None, :], (length, choose, width)).reshape(
        length * choose, width
    )
    routed_ids = jnp.broadcast_to(sentence[:, None], (length, choose)).reshape(length * choose)
    dispatch_rows = (
        jnp.zeros((experts * capacity, width), jnp.bfloat16)
        .at[slot_index]
        .set(routed_rows)
        .reshape(experts, capacity, width)
    )
    dispatch_ids = (
        jnp.full((experts * capacity,), -1, jnp.int32)
        .at[slot_index]
        .set(routed_ids)
        .reshape(experts, capacity)
    )
    arrived, arrived_ids = (
        lax.all_to_all(dispatch_rows, "expert", split_axis=0, concat_axis=0, tiled=True),
        lax.all_to_all(dispatch_ids, "expert", split_axis=0, concat_axis=0, tiled=True),
    )
    all_shared, all_ids = (
        lax.all_gather(shared, "expert", axis=0, tiled=True),
        lax.all_gather(sentence, "expert", axis=0, tiled=True),
    )
    all_shared = all_shared.reshape(experts, length, 2 * head_size)
    all_ids = all_ids.reshape(experts, length)
    own_query = w_query[0]
    own_output = w_output[0]

    def forward_item(item):
        rows, row_ids, item_shared, key_ids = item
        return head_forward(rows, row_ids, item_shared, key_ids, own_query, own_output)

    results, kept_queries, kept_attended, kept_totals = lax.map(
        forward_item, (arrived, arrived_ids, all_shared, all_ids)
    )
    returned = lax.all_to_all(results, "expert", split_axis=0, concat_axis=0, tiled=True)
    returned_rows = (
        returned.reshape(experts * capacity, width)[slot_index]
        .astype(jnp.float32)
        .reshape(length, choose, width)
    )
    mixed = jnp.sum(gates[:, :, None] * returned_rows, axis=1)
    hidden_in = inputs + mixed
    normed_two, norm_two, inverse_two = layer_norm_parts(hidden_in, ln_ffn)
    normed_two_low = normed_two.astype(jnp.bfloat16)
    before = product(normed_two_low, w_in)
    activated = gelu_exact(before).astype(jnp.bfloat16)
    output = (hidden_in + product(activated, w_out)).astype(jnp.bfloat16)
    out_weight_grad = product_tn(activated, out_grad)
    activated_grad = product_nt(out_grad, w_out)
    before_grad = (activated_grad * gelu_slope(before)).astype(jnp.bfloat16)
    in_weight_grad = product_tn(normed_two_low, before_grad)
    normed_two_grad = product_nt(before_grad, w_in)
    hidden_back, ln_ffn_grad = layer_norm_back(normed_two_grad, norm_two, inverse_two, ln_ffn)
    hidden_grad = out_grad.astype(jnp.float32) + hidden_back
    gate_grad = jnp.sum(hidden_grad[:, None, :] * returned_rows, axis=2)
    picked_grad = gates * (gate_grad - jnp.sum(gates * gate_grad, axis=-1, keepdims=True))
    logits_grad = jnp.sum(selector * picked_grad[:, :, None], axis=1).astype(jnp.bfloat16)
    router_grad = product_tn(normed_low, logits_grad)
    route_grad = (
        (gates[:, :, None] * hidden_grad[:, None, :])
        .astype(jnp.bfloat16)
        .reshape(length * choose, width)
    )
    route_dispatch = (
        jnp.zeros((experts * capacity, width), jnp.bfloat16)
        .at[slot_index]
        .set(route_grad)
        .reshape(experts, capacity, width)
    )
    arrived_grad = lax.all_to_all(route_dispatch, "expert", split_axis=0, concat_axis=0, tiled=True)

    def backward_item(item):
        rows, row_ids, item_shared, key_ids, queries, attended, totals, result_grad = item
        return head_backward(
            rows,
            row_ids,
            item_shared,
            key_ids,
            own_query,
            own_output,
            queries,
            attended,
            totals,
            result_grad,
        )

    rows_grad, shared_parts, query_parts, output_parts = lax.map(
        backward_item,
        (
            arrived,
            arrived_ids,
            all_shared,
            all_ids,
            kept_queries,
            kept_attended,
            kept_totals,
            arrived_grad,
        ),
    )
    back_rows = lax.all_to_all(rows_grad, "expert", split_axis=0, concat_axis=0, tiled=True)
    shared_grad = lax.psum_scatter(
        shared_parts.reshape(experts * length, 2 * head_size).astype(jnp.bfloat16),
        "expert",
        scatter_dimension=0,
        tiled=True,
    )
    query_grad_sum = jnp.sum(query_parts, axis=0)[None]
    output_grad_sum = jnp.sum(output_parts, axis=0)[None]
    query_total, output_total = (
        lax.psum(query_grad_sum.astype(jnp.bfloat16), ("dp", "tok")).astype(jnp.float32),
        lax.psum(output_grad_sum.astype(jnp.bfloat16), ("dp", "tok")).astype(jnp.float32),
    )
    kv_weight_grad = product_tn(normed_low, shared_grad)
    routes_back = (
        back_rows.reshape(experts * capacity, width)[slot_index]
        .astype(jnp.float32)
        .reshape(length, choose, width)
    )
    normed_grad = (
        product_nt(shared_grad, w_kv)
        + product_nt(logits_grad, w_router)
        + jnp.sum(routes_back, axis=1)
    )
    input_back, ln_attn_grad = layer_norm_back(normed_grad, norm_one, inverse_one, ln_attn)
    input_grad = (hidden_grad + input_back).astype(jnp.bfloat16)
    summed = lax.psum(
        (ln_attn_grad, kv_weight_grad, router_grad, in_weight_grad, out_weight_grad, ln_ffn_grad),
        ("dp", "expert", "tok"),
    )
    return (
        output,
        input_grad,
        summed[0],
        summed[1],
        summed[2],
        query_total,
        output_total,
        summed[5],
        summed[3],
        summed[4],
    )


def solution(mesh):
    return jax.shard_map(
        body,
        mesh=mesh,
        in_specs=(
            P(("dp", "expert", "tok"), None),
            P(("dp", "expert", "tok"), None),
            P(("dp", "expert", "tok"), None),
            P(("dp", "expert", "tok"), None),
            P(),
            P(),
            P(),
            P("expert", None, None),
            P("expert", None, None),
            P(),
            P(),
            P(),
        ),
        out_specs=(
            P(("dp", "expert", "tok"), None),
            P(("dp", "expert", "tok"), None),
            P(),
            P(),
            P(),
            P("expert", None, None),
            P("expert", None, None),
            P(),
            P(),
            P(),
        ),
        check_vma=False,
    )
```

profile of v0, /device:TPU:0, one launch (start us, length us, event | category | flops | bytes accessed | tf_op | source)
XLA Modules:
  0.0 818.5 jit_solution(17089918963078222424)
XLA Ops:
  19.5 8.6 %scatter_custom_fusion = s32[3072]{0:T(1024)} fusion(s32[2048]{0:T(1024)S(1)} %bitcast.203, s32[2048]{0:T(1024)S(1)} %reshape.331, s32[]{:T(128)} %constant.101.clone.1), kind=kCustom, calls=%fused_computation.137 | custom fusion | bytes 12292 | tf_op jit(solution)/shard_map/scatter | solution.py:149
  28.2 6.3 all-to-all-start
  40.0 4.1 reshape.339
  44.1 12.1 %scatter_custom_fusion.1 = bf16[3072,512]{1,0:T(8,128)(2,1)} fusion(s32[2048]{0:T(1024)S(1)} %bitcast.204, bf16[2048,512]{1,0:T(8,128)(2,1)} %reshape.339, bf16[]{:T(256)} %constant.98.clone.1), kind=kCustom, calls=%fused_computation.115 | custom fusion | bytes 3146240 | tf_op jit(solution)/shard_map/scatter | solution.py:143
  56.1 5.2 all-to-all-start.1
  62.6 91.3 %all-gather = s32[1,4096]{1,0:T(1,128)S(1)} all-gather(s32[1,1024]{1,0:T(1,128)S(1)} %copy-done.35), channel_id=2, replica_groups=mesh['dp'=4,'expert'=4,'tok'=2] {'expert'}, dimensions={1}, use_global_device_ids=true | all-gather | bytes 20480 | tf_op jit(solution)/shard_map/all_gather | solution.py:158
  157.8 41.3 %while.32 = (s32[]{:T(128)}, bf16[4,768,512]{2,1,0:T(8,128)(2,1)}, bf16[4,768,64]{1,2,0:T(8,128)(2,1)}, bf16[4,768,64]{1,2,0:T(8,128)(2,1)}, f32[4,768]{1,0:T(4,...) while((s32[]{:T(128)}, bf16[4,768,512]{2,1,0:T(8,128)(2,1)}, ...), condition=%wide.region_13.14_spmd, body=%wide.region_10.13_spmd.sunk | while | flops 314277120 | bytes 12918941 | solution.py:169
  199.1 4.8 all-to-all-start.2
  204.9 66.7 %all-to-all-done.2 = bf16[4,768,512]{2,1,0:T(8,128)(2,1)} async-done(((bf16[4,768,512]{2,1,0:T(8,128)(2,1)}), bf16[4,768,512]{2,1,0:T(8,128)(2,1)}, u32[]{:S(2)}, u32[]{:S(2)}) %all-to-all-start.2) | async-done | bytes 3145760 | tf_op jit(solution)/shard_map/all_to_all | solution.py:172
  271.6 11.6 %gather_fusion = bf16[2048,512]{1,0:T(8,128)(2,1)} fusion(bf16[3072,512]{1,0:T(8,128)(2,1)} %bitcast.25, s32[2048]{0:T(1024)S(1)} %broadcast_clamp_fusion), kind=kCustom, calls=%fused_computation | custom fusion | bytes 4202496 | tf_op jit(solution)/shard_map/gather | solution.py:174
  283.2 5.4 reshape.309
  288.6 7.7 multiply_reduce_fusion.2
  297.1 4.7 multiply_convert_fusion.1
  301.8 5.0 fusion.47
  316.2 6.2 mul.257
  322.5 13.1 %scatter_custom_fusion.2 = bf16[3072,512]{1,0:T(8,128)(2,1)} fusion(s32[2048]{0:T(1024)S(1)} %bitcast.206, f32[2048,512]{1,0:T(8,128)} %mul.257, f32[2048]{0:T(1024)S(1)} %div.59, bf16[]{:T(256)} %constant.98.clone.1), kind=kCustom, calls=%fused_computation.102 | custom fusion | flops 2097152 | bytes 7348226 | tf_op jit(solution)/shard_map/scatter | solution.py:204
  339.4 70.0 %all-to-all-done.3 = bf16[4,768,512]{2,1,0:T(8,128)(2,1)S(1)} async-done(((bf16[4,768,512]{2,1,0:T(8,128)(2,1)}), bf16[4,768,512]{2,1,0:T(8,128)(2,1)S(1)}, u32[]{:S(2)}, u32[]{:S(2)}) %all-to-all-start.3) | async-done | bytes 3145760 | tf_op jit(solution)/shard_map/all_to_all | solution.py:207
  411.3 68.2 %while.33 = (s32[]{:T(128)}, bf16[4,768,512]{2,1,0:T(8,128)(2,1)}, bf16[4,1024,128]{2,1,0:T(8,128)(2,1)}, f32[4,512,64]{1,2,0:T(8,128)}, f32[4,64,512]{2,1,0:T(8...) while((s32[]{:T(128)}, bf16[4,768,512]{2,1,0:T(8,128)(2,1)}, ...), condition=%wide.region_22.23_spmd, body=%wide.region_20.22_spmd.sunk | while | flops 713702656 | bytes 31267520 | solution.py:224
  479.6 3.7 all-to-all-start.4
  483.8 7.2 fusion.84
  491.0 4.6 fusion.78
  499.1 30.9 %reduce-scatter.2.cloned.1.call-done = bf16[1024,128]{1,0:T(8,128)(2,1)} async-done(((bf16[4096,128]{1,0:T(8,128)(2,1)}), bf16[1024,128]{1,0:T(8,128)(2,1)}) %reduce-scatter.2.cloned.1.call-update) | async-done | bytes 262160 | tf_op jit(solution)/shard_map/reduce_scatter | solution.py:238
  532.5 5.9 multiply_reduce_fusion.1
  541.8 6.8 add_convert_fusion
  548.6 64.8 %all-reduce.8.cloned.1.call-done = (bf16[1,512,64]{1,2,0:T(8,128)(2,1)}, bf16[1,64,512]{2,1,0:T(8,128)(2,1)}) async-done(((bf16[1,512,64]{1,2,0:T(8,128)(2,1)}, bf16[1,64,512]{2,1,0:T(8,128)(2,1)}), (bf16[1,512,64]{1,2,0:T(8,128)(2,1)}, bf16[1,64,512]{2,1,0:T(8,128)(2,1)})) %all-reduce.8.cloned.1.call-update) | async-done | bytes 131088 | tf_op jit(solution)/shard_map/psum | solution.py:247
  618.2 9.4 %gather_fusion.1 = bf16[2048,512]{1,0:T(8,128)(2,1)} fusion(bf16[3072,512]{1,0:T(8,128)(2,1)S(1)} %bitcast.191, s32[2048]{0:T(1024)S(1)} %copy-done.22), kind=kCustom, calls=%fused_computation.1 | custom fusion | bytes 4202496 | tf_op jit(solution)/shard_map/gather | solution.py:252
  627.6 5.5 reshape.310
  633.1 8.7 %reduce_sum.214 = f32[1024,512]{1,0:T(8,128)} reduce(f32[1024,2,512]{2,1,0:T(2,128)} %reshape.310, f32[]{:T(128)} %constant.71.clone.1), dimensions={1}, to_apply=%region_27.28 | reduce | flops 524288 | bytes 6291460 | tf_op jit(solution)/shard_map/reduce_sum | solution.py:259
  641.9 4.8 fusion.60
  646.7 40.1 %all-reduce = (f32[512]{0:T(512)}, f32[512,4]{0,1:T(4,128)}, f32[512]{0:T(512)}) all-reduce(f32[512]{0:T(512)S(1)} %get-tuple-element.235, f32[512,4]{0,1:T(4,128)S(1)} %copy-done.28, f32[512]{0:T(512)S(1)} %copy-done.36), channel_id=1, replica_groups=mesh['dp'=4,'expert'=4,'tok'=2] {'dp','expert','tok'}, use_global_device_ids=true, to_apply=%region_31.32 | all-reduce | flops 3072 | bytes 24576 | tf_op jit(solution)/shard_map/psum | solution.py:263
  689.9 113.4 %all-reduce.6.cloned.1.call-done = (f32[512,128]{1,0:T(8,128)}, f32[512,2048]{1,0:T(8,128)}, f32[2048,512]{1,0:T(8,128)}) async-done(((f32[512,128]{1,0:T(8,128)}, f32[512,2048]{1,0:T(8,128)}, f32[2048,512]{1,0:T(8,128)}), (f32[512,128]{1,0:T(8,128)}, f32[512,2048]{1,0:T(8,128)}, f32[2048,512]{1,0:T(8,128)})) %all-reduce.6.cloned.1.call-update) | async-done | bytes 8650768 | tf_op jit(solution)/shard_map/psum | solution.py:263
  805.0 4.8 copy.166
  (268 shorter events, 170.1 us)
Async XLA Ops:
  7.2 289.8 %copy-start = (bf16[512,2048]{1,0:T(8,128)(2,1)S(1)}, bf16[512,2048]{1,0:T(8,128)(2,1)}, u32[]{:S(2)}) copy-start(bf16[512,2048]{1,0:T(8,128)(2,1)} %param.26) | copy-start | bytes 6291460
  7.2 27.3 %copy-start.5 = (bf16[1024,512]{1,0:T(8,128)(2,1)S(1)}, bf16[1024,512]{1,0:T(8,128)(2,1)}, u32[]{:S(2)}) copy-start(bf16[1024,512]{1,0:T(8,128)(2,1)} %param.16) | copy-start | bytes 3145732
  7.2 28.7 %copy-start.29 = (f32[512]{0:T(512)S(1)}, f32[512]{0:T(512)}, u32[]{:S(2)}) copy-start(f32[512]{0:T(512)} %param.20) | copy-start | bytes 6148
  28.2 28.0 %all-to-all-start = ((s32[4,1,768]{2,1,0:T(1,128)}), s32[4,1,768]{2,1,0:T(1,128)S(1)}, u32[]{:S(2)}, u32[]{:S(2)}) async-start(s32[4,1,768]{2,1,0:T(1,128)} %bitcast.20), calls=%async_computation | async-start | bytes 24576 | tf_op jit(solution)/shard_map/all_to_all | solution.py:154
  37.5 166.3 %copy-start.4 = (bf16[1024,512]{1,0:T(8,128)(2,1)}, bf16[1024,512]{1,0:T(8,128)(2,1)S(1)}, u32[]{:S(2)}) copy-start(bf16[1024,512]{1,0:T(8,128)(2,1)S(1)} %fusion.54) | copy-start | bytes 3145732
  56.1 99.0 %copy-start.25 = (bf16[1,512,64]{1,2,0:T(8,128)(2,1)S(1)}, bf16[1,512,64]{1,2,0:T(8,128)(2,1)}, u32[]{:S(2)}) copy-start(bf16[1,512,64]{1,2,0:T(8,128)(2,1)} %param.23) | copy-start | bytes 196612
  56.1 99.7 %all-to-all-start.1 = ((bf16[4,768,512]{2,1,0:T(8,128)(2,1)}), bf16[4,768,512]{2,1,0:T(8,128)(2,1)}, u32[]{:S(2)}, u32[]{:S(2)}) async-start(bf16[4,768,512]{2,1,0:T(8,128)(2,1)} %bitcast.192), calls=%async_computation.1 | async-start | bytes 6291456 | tf_op jit(solution)/shard_map/all_to_all | solution.py:153
  61.4 94.5 %all-gather.3.cloned.1.call-start = ((), (), s32[]{:S(2)}) async-start(), calls=%async_computation.6 | async-start | bytes 1310720 | tf_op jit(solution)/shard_map/all_gather | solution.py:157
  199.1 72.5 %all-to-all-start.2 = ((bf16[4,768,512]{2,1,0:T(8,128)(2,1)}), bf16[4,768,512]{2,1,0:T(8,128)(2,1)}, u32[]{:S(2)}, u32[]{:S(2)}) async-start(bf16[4,768,512]{2,1,0:T(8,128)(2,1)} %get-tuple-element.150), calls=%async_computation.2 | async-start | bytes 6291456 | tf_op jit(solution)/shard_map/all_to_all | solution.py:172
  204.4 78.8 %copy-start.26 = (f32[1024]{0:T(1024)}, f32[1024]{0:T(1024)S(1)}, u32[]{:S(2)}) copy-start(f32[1024]{0:T(1024)S(1)} %fusion.74) | copy-start | bytes 12292
  204.9 78.2 %copy-start.21 = (s32[2048]{0:T(1024)}, s32[2048]{0:T(1024)S(1)}, u32[]{:S(2)}) copy-start(s32[2048]{0:T(1024)S(1)} %broadcast_clamp_fusion) | copy-start | bytes 24580
  288.6 7.7 copy-start.6
  296.6 13.7 %copy-start.2 = (f32[1024,512]{1,0:T(8,128)}, f32[1024,512]{1,0:T(8,128)S(1)}, u32[]{:S(2)}) copy-start(f32[1024,512]{1,0:T(8,128)S(1)} %get-tuple-element.300) | copy-start | bytes 6291460
  335.6 73.8 %all-to-all-start.3 = ((bf16[4,768,512]{2,1,0:T(8,128)(2,1)}), bf16[4,768,512]{2,1,0:T(8,128)(2,1)S(1)}, u32[]{:S(2)}, u32[]{:S(2)}) async-start(bf16[4,768,512]{2,1,0:T(8,128)(2,1)} %bitcast.193), calls=%async_computation.3 | async-start | bytes 6291456 | tf_op jit(solution)/shard_map/all_to_all | solution.py:207
  339.3 190.7 %reduce-scatter.2.cloned.1.call-start = ((), (), s32[]{:S(2)}) async-start(), calls=%async_computation.7 | async-start | bytes 1310720 | tf_op jit(solution)/shard_map/reduce_scatter | solution.py:238
  479.6 138.6 %all-to-all-start.4 = ((bf16[4,768,512]{2,1,0:T(8,128)(2,1)}), bf16[4,768,512]{2,1,0:T(8,128)(2,1)S(1)}, u32[]{:S(2)}, u32[]{:S(2)}) async-start(bf16[4,768,512]{2,1,0:T(8,128)(2,1)} %get-tuple-element.155), calls=%async_computation.5 | async-start | bytes 6291456 | tf_op jit(solution)/shard_map/all_to_all | solution.py:237
  483.3 130.1 %all-reduce.8.cloned.1.call-start = ((), (), s32[]{:S(2)}) async-start(), calls=%async_computation.9 | async-start | bytes 262144 | tf_op jit(solution)/shard_map/psum | solution.py:247
  483.8 7.2 copy-start.3
  483.8 7.2 copy-start.11
  483.8 7.2 copy-start.32
  499.0 304.3 %all-reduce.6.cloned.1.call-start = ((), (), s32[]{:S(2)}) async-start(), calls=%async_computation.8 | async-start | bytes 17301504 | tf_op jit(solution)/shard_map/psum | solution.py:263
  532.4 7.2 copy-start.27
  532.4 7.2 copy-start.18
  541.8 74.6 %copy-start.13 = (bf16[1024,128]{1,0:T(8,128)(2,1)S(1)}, bf16[1024,128]{1,0:T(8,128)(2,1)}, u32[]{:S(2)}) copy-start(bf16[1024,128]{1,0:T(8,128)(2,1)} %reduce-scatter.2.cloned.1.call-done) | copy-start | bytes 786436
  541.8 74.6 %copy-start.16 = (bf16[512,128]{1,0:T(8,128)(2,1)S(1)}, bf16[512,128]{1,0:T(8,128)(2,1)}, u32[]{:S(2)}) copy-start(bf16[512,128]{1,0:T(8,128)(2,1)} %param.21) | copy-start | bytes 393220
  541.8 76.4 %copy-start.22 = (s32[2048]{0:T(1024)S(1)}, s32[2048]{0:T(1024)}, u32[]{:S(2)}) copy-start(s32[2048]{0:T(1024)} %copy-done.21) | copy-start | bytes 24580
  633.1 8.7 %copy-start.7 = (bf16[1024,512]{1,0:T(8,128)(2,1)S(1)}, bf16[1024,512]{1,0:T(8,128)(2,1)}, u32[]{:S(2)}) copy-start(bf16[1024,512]{1,0:T(8,128)(2,1)} %param.16) | copy-start | bytes 3145732
  633.1 8.7 %copy-start.20 = (f32[1024]{0:T(1024)S(1)}, f32[1024]{0:T(1024)}, u32[]{:S(2)}) copy-start(f32[1024]{0:T(1024)} %copy-done.19) | copy-start | bytes 12292
  633.1 8.7 %copy-start.24 = (f32[1024]{0:T(1024)S(1)}, f32[1024]{0:T(1024)}, u32[]{:S(2)}) copy-start(f32[1024]{0:T(1024)} %copy-done.23) | copy-start | bytes 12292
  633.1 8.7 %copy-start.30 = (f32[512]{0:T(512)S(1)}, f32[512]{0:T(512)}, u32[]{:S(2)}) copy-start(f32[512]{0:T(512)} %param.20) | copy-start | bytes 6148
  633.1 8.7 %copy-start.34 = (bf16[512,4]{0,1:T(4,128)(2,1)S(1)}, bf16[512,4]{0,1:T(4,128)(2,1)}, u32[]{:S(2)}) copy-start(bf16[512,4]{0,1:T(4,128)(2,1)} %param.22) | copy-start | bytes 12292
  641.9 45.0 %copy-start.9 = (f32[1024,512]{1,0:T(8,128)S(1)}, f32[1024,512]{1,0:T(8,128)}, u32[]{:S(2)}) copy-start(f32[1024,512]{1,0:T(8,128)} %copy-done.8) | copy-start | bytes 6291460
  (15 other events, 59.3 us)
Sparse Core Ops, SparseCore 0:
  64.3 43.4 all-gather.2
  479.7 50.2 reduce-scatter.1
  533.9 79.4 all-reduce.7
  620.0 183.2 all-reduce.5
where the time goes:
time: 829 us; the launch traced here: 819 us
  waiting for transfers between devices  346 us (42%)
  blocking collectives  131 us (16%)
  matrix products  122 us (15%)
  local copies, waits for them, and re-layouts  120 us (14%)
  other arithmetic  60.4 us (7%)
  starting transfers between devices  24.3 us (3%)
  between operations  14.5 us (2%)
    psum x1, waiting for transfers between devices, body(): lax.psum((ln_attn_grad, kv_weight_grad, router_grad, in_weight_grad, out_...  113 us
    all_gather x1, blocking collectives, body(): lax.all_gather(sentence, 'expert', axis=0, tiled=True)  91.3 us
    all_to_all x1, waiting for transfers between devices, body(): lax.all_to_all(route_dispatch, 'expert', split_axis=0, concat_axis=0, til...  70 us
    all_to_all x1, waiting for transfers between devices, body(): lax.all_to_all(results, 'expert', split_axis=0, concat_axis=0, tiled=True)  66.7 us
    psum x1, waiting for transfers between devices, body(): lax.psum(query_grad_sum.astype(jnp.bfloat16), ('dp', 'tok'))  64.8 us
    dot_general x24, matrix products, product_nt(): lax.dot_general(left, right, (((1,), (1,)), ((), ())), preferred_element_...  43.4 us
    dot_general x20, matrix products, product(): return jnp.dot(left, right, preferred_element_type=jnp.float32)  40.2 us
    psum x1, blocking collectives, body(): lax.psum((ln_attn_grad, kv_weight_grad, router_grad, in_weight_grad, out_...  40.1 us
  transfers between devices with their start and end apart: 9, of which 5 were waited for; matrix products, arithmetic and copies ran while one was open for 12% of the time, Pallas kernels for 0%

commit v1 on v0

--- a/solution.py
+++ b/solution.py
@@ -244,7 +244,9 @@
     query_grad_sum = jnp.sum(query_parts, axis=0)[None]
     output_grad_sum = jnp.sum(output_parts, axis=0)[None]
     query_total, output_total = (
-        lax.psum(query_grad_sum.astype(jnp.bfloat16), ("dp", "tok")).astype(jnp.float32),
+        jnp.sum(lax.all_gather(query_grad_sum.astype(jnp.bfloat16), ("dp", "tok")), axis=0).astype(
+            jnp.float32
+        ),
         lax.psum(output_grad_sum.astype(jnp.bfloat16), ("dp", "tok")).astype(jnp.float32),
     )
     kv_weight_grad = product_tn(normed_low, shared_grad)

time: 829 us -> 827 us (level)
  blocking collectives: 131 us -> 142 us
  waiting for transfers between devices: 346 us -> 335 us
    psum x1, waiting for transfers between devices: 64.8 us -> 50.4 us  [body(): lax.psum(output_grad_sum.astype(jnp.bfloat16), ('dp', 'tok'))]
    all_gather x0 -> x1, blocking collectives: none -> 10.2 us  [body(): lax.all_gather(query_grad_sum.astype(jnp.bfloat16), ('dp', 'tok'))]
where the time goes in v1:
time: 827 us; the launch traced here: 816 us
  waiting for transfers between devices  335 us (41%)
  blocking collectives  142 us (17%)
  matrix products  122 us (15%)
  local copies, waits for them, and re-layouts  118 us (14%)
  other arithmetic  60.1 us (7%)
  starting transfers between devices  24.3 us (3%)
  between operations  14.5 us (2%)
    psum x1, waiting for transfers between devices, body(): lax.psum((ln_attn_grad, kv_weight_grad, router_grad, in_weight_grad, out_...  115 us
    all_gather x1, blocking collectives, body(): lax.all_gather(sentence, 'expert', axis=0, tiled=True)  91.3 us
    all_to_all x1, waiting for transfers between devices, body(): lax.all_to_all(route_dispatch, 'expert', split_axis=0, concat_axis=0, til...  70 us
    all_to_all x1, waiting for transfers between devices, body(): lax.all_to_all(results, 'expert', split_axis=0, concat_axis=0, tiled=True)  66.7 us
    psum x1, waiting for transfers between devices, body(): lax.psum(output_grad_sum.astype(jnp.bfloat16), ('dp', 'tok'))  50.4 us
    dot_general x24, matrix products, product_nt(): lax.dot_general(left, right, (((1,), (1,)), ((), ())), preferred_element_...  43.3 us
    psum x1, blocking collectives, body(): lax.psum((ln_attn_grad, kv_weight_grad, router_grad, in_weight_grad, out_...  40.4 us
    dot_general x20, matrix products, product(): return jnp.dot(left, right, preferred_element_type=jnp.float32)  40.2 us
  transfers between devices with their start and end apart: 9, of which 5 were waited for; matrix products, arithmetic and copies ran while one was open for 12% of the time, Pallas kernels for 0%

profile of v1, /device:TPU:0, one launch (start us, length us, event | category | flops | bytes accessed | tf_op | source)
XLA Modules:
  0.0 816.3 jit_solution(12655800114792666825)
XLA Ops:
  19.5 8.6 %scatter_custom_fusion = s32[3072]{0:T(1024)} fusion(s32[2048]{0:T(1024)S(1)} %bitcast.208, s32[2048]{0:T(1024)S(1)} %reshape.344, s32[]{:T(128)} %constant.102.clone.1), kind=kCustom, calls=%fused_computation.138 | custom fusion | bytes 12292 | tf_op jit(solution)/shard_map/scatter | solution.py:149
  28.2 6.3 all-to-all-start
  40.0 4.1 reshape.352
  44.1 12.1 %scatter_custom_fusion.1 = bf16[3072,512]{1,0:T(8,128)(2,1)} fusion(s32[2048]{0:T(1024)S(1)} %bitcast.209, bf16[2048,512]{1,0:T(8,128)(2,1)} %reshape.352, bf16[]{:T(256)} %constant.99.clone.1), kind=kCustom, calls=%fused_computation.115 | custom fusion | bytes 3146240 | tf_op jit(solution)/shard_map/scatter | solution.py:143
  56.1 5.2 all-to-all-start.1
  62.6 91.3 %all-gather = s32[1,4096]{1,0:T(1,128)S(1)} all-gather(s32[1,1024]{1,0:T(1,128)S(1)} %copy-done.36), channel_id=2, replica_groups=mesh['dp'=4,'expert'=4,'tok'=2] {'expert'}, dimensions={1}, use_global_device_ids=true | all-gather | bytes 20480 | tf_op jit(solution)/shard_map/all_gather | solution.py:158
  157.8 41.4 %while.32 = (s32[]{:T(128)}, bf16[4,768,512]{2,1,0:T(8,128)(2,1)}, bf16[4,768,64]{1,2,0:T(8,128)(2,1)}, bf16[4,768,64]{1,2,0:T(8,128)(2,1)}, f32[4,768]{1,0:T(4,...) while((s32[]{:T(128)}, bf16[4,768,512]{2,1,0:T(8,128)(2,1)}, ...), condition=%wide.region_13.14_spmd, body=%wide.region_10.13_spmd.sunk | while | flops 314277120 | bytes 12918941 | solution.py:169
  199.2 4.8 all-to-all-start.2
  205.0 66.7 %all-to-all-done.2 = bf16[4,768,512]{2,1,0:T(8,128)(2,1)} async-done(((bf16[4,768,512]{2,1,0:T(8,128)(2,1)}), bf16[4,768,512]{2,1,0:T(8,128)(2,1)}, u32[]{:S(2)}, u32[]{:S(2)}) %all-to-all-start.2) | async-done | bytes 3145760 | tf_op jit(solution)/shard_map/all_to_all | solution.py:172
  271.7 11.6 %gather_fusion = bf16[2048,512]{1,0:T(8,128)(2,1)} fusion(bf16[3072,512]{1,0:T(8,128)(2,1)} %bitcast.25, s32[2048]{0:T(1024)S(1)} %broadcast_clamp_fusion), kind=kCustom, calls=%fused_computation | custom fusion | bytes 4202496 | tf_op jit(solution)/shard_map/gather | solution.py:174
  283.2 5.4 reshape.321
  288.7 7.7 multiply_reduce_fusion.2
  297.2 4.7 multiply_convert_fusion.1
  301.9 5.0 fusion.47
  314.9 6.2 mul.257
  321.2 13.1 %scatter_custom_fusion.2 = bf16[3072,512]{1,0:T(8,128)(2,1)} fusion(s32[2048]{0:T(1024)S(1)} %bitcast.211, f32[2048,512]{1,0:T(8,128)} %mul.257, f32[2048]{0:T(1024)S(1)} %div.59, bf16[]{:T(256)} %constant.99.clone.1), kind=kCustom, calls=%fused_computation.102 | custom fusion | flops 2097152 | bytes 7348226 | tf_op jit(solution)/shard_map/scatter | solution.py:204
  338.1 70.0 %all-to-all-done.3 = bf16[4,768,512]{2,1,0:T(8,128)(2,1)S(1)} async-done(((bf16[4,768,512]{2,1,0:T(8,128)(2,1)}), bf16[4,768,512]{2,1,0:T(8,128)(2,1)S(1)}, u32[]{:S(2)}, u32[]{:S(2)}) %all-to-all-start.3) | async-done | bytes 3145760 | tf_op jit(solution)/shard_map/all_to_all | solution.py:207
  410.0 68.2 %while.33 = (s32[]{:T(128)}, bf16[4,768,512]{2,1,0:T(8,128)(2,1)}, bf16[4,1024,128]{2,1,0:T(8,128)(2,1)}, f32[4,512,64]{1,2,0:T(8,128)}, f32[4,64,512]{2,1,0:T(8...) while((s32[]{:T(128)}, bf16[4,768,512]{2,1,0:T(8,128)(2,1)}, ...), condition=%wide.region_22.23_spmd, body=%wide.region_20.22_spmd.sunk | while | flops 713702656 | bytes 31267520 | solution.py:224
  482.5 7.2 fusion.84
  489.7 4.6 fusion.78
  496.1 32.6 %reduce-scatter.2.cloned.1.call-done = bf16[1024,128]{1,0:T(8,128)(2,1)} async-done(((bf16[4096,128]{1,0:T(8,128)(2,1)}), bf16[1024,128]{1,0:T(8,128)(2,1)}) %reduce-scatter.2.cloned.1.call-update) | async-done | bytes 262160 | tf_op jit(solution)/shard_map/reduce_scatter | solution.py:238
  531.2 5.9 multiply_reduce_fusion.1
  540.5 6.7 add_convert_fusion
  549.1 10.2 %all-gather.1 = bf16[4096,64]{0,1:T(8,128)(2,1)S(1)} all-gather(bf16[512,64]{0,1:T(8,128)(2,1)} %reduce_sum.230), channel_id=3, replica_groups=mesh['dp'=4,'expert'=4,'tok'=2] {'dp','tok'}, dimensions={0}, use_global_device_ids=true | all-gather | bytes 589824 | tf_op jit(solution)/shard_map/all_gather | solution.py:247
  560.5 50.4 %all-reduce.5.cloned.1.call-done = bf16[1,64,512]{2,1,0:T(8,128)(2,1)} async-done(((bf16[1,64,512]{2,1,0:T(8,128)(2,1)}), bf16[1,64,512]{2,1,0:T(8,128)(2,1)}) %all-reduce.5.cloned.1.call-update) | async-done | bytes 65552 | tf_op jit(solution)/shard_map/psum | solution.py:250
  614.3 9.2 %gather_fusion.1 = bf16[2048,512]{1,0:T(8,128)(2,1)} fusion(bf16[3072,512]{1,0:T(8,128)(2,1)S(1)} %bitcast.196, s32[2048]{0:T(1024)S(1)} %copy-done.23), kind=kCustom, calls=%fused_computation.1 | custom fusion | bytes 4202496 | tf_op jit(solution)/shard_map/gather | solution.py:254
  623.5 5.5 reshape.322
  628.9 8.7 %reduce_sum.226 = f32[1024,512]{1,0:T(8,128)} reduce(f32[1024,2,512]{2,1,0:T(2,128)} %reshape.322, f32[]{:T(128)} %constant.94.clone.1), dimensions={1}, to_apply=%region_27.28 | reduce | flops 524288 | bytes 6291460 | tf_op jit(solution)/shard_map/reduce_sum | solution.py:261
  637.7 4.8 fusion.60
  642.5 40.4 %all-reduce = (f32[512]{0:T(512)}, f32[512,4]{0,1:T(4,128)}, f32[512]{0:T(512)}) all-reduce(f32[512]{0:T(512)S(1)} %get-tuple-element.235, f32[512,4]{0,1:T(4,128)S(1)} %copy-done.29, f32[512]{0:T(512)S(1)} %copy-done.37), channel_id=1, replica_groups=mesh['dp'=4,'expert'=4,'tok'=2] {'dp','expert','tok'}, use_global_device_ids=true, to_apply=%region_31.32 | all-reduce | flops 3072 | bytes 24576 | tf_op jit(solution)/shard_map/psum | solution.py:265
  686.0 115.1 %all-reduce.7.cloned.1.call-done = (f32[512,128]{1,0:T(8,128)}, f32[512,2048]{1,0:T(8,128)}, f32[2048,512]{1,0:T(8,128)}) async-done(((f32[512,128]{1,0:T(8,128)}, f32[512,2048]{1,0:T(8,128)}, f32[2048,512]{1,0:T(8,128)}), (f32[512,128]{1,0:T(8,128)}, f32[512,2048]{1,0:T(8,128)}, f32[2048,512]{1,0:T(8,128)})) %all-reduce.7.cloned.1.call-update) | async-done | bytes 8650768 | tf_op jit(solution)/shard_map/psum | solution.py:265
  802.7 4.8 copy.166
  (273 shorter events, 172.3 us)
Async XLA Ops:
  7.2 290.0 %copy-start = (bf16[512,2048]{1,0:T(8,128)(2,1)S(1)}, bf16[512,2048]{1,0:T(8,128)(2,1)}, u32[]{:S(2)}) copy-start(bf16[512,2048]{1,0:T(8,128)(2,1)} %param.26) | copy-start | bytes 6291460
  7.2 27.3 %copy-start.5 = (bf16[1024,512]{1,0:T(8,128)(2,1)S(1)}, bf16[1024,512]{1,0:T(8,128)(2,1)}, u32[]{:S(2)}) copy-start(bf16[1024,512]{1,0:T(8,128)(2,1)} %param.16) | copy-start | bytes 3145732
  7.2 28.7 %copy-start.30 = (f32[512]{0:T(512)S(1)}, f32[512]{0:T(512)}, u32[]{:S(2)}) copy-start(f32[512]{0:T(512)} %param.20) | copy-start | bytes 6148
  28.2 28.0 %all-to-all-start = ((s32[4,1,768]{2,1,0:T(1,128)}), s32[4,1,768]{2,1,0:T(1,128)S(1)}, u32[]{:S(2)}, u32[]{:S(2)}) async-start(s32[4,1,768]{2,1,0:T(1,128)} %bitcast.20), calls=%async_computation | async-start | bytes 24576 | tf_op jit(solution)/shard_map/all_to_all | solution.py:154
  37.5 166.4 %copy-start.4 = (bf16[1024,512]{1,0:T(8,128)(2,1)}, bf16[1024,512]{1,0:T(8,128)(2,1)S(1)}, u32[]{:S(2)}) copy-start(bf16[1024,512]{1,0:T(8,128)(2,1)S(1)} %fusion.54) | copy-start | bytes 3145732
  56.1 99.0 %copy-start.26 = (bf16[1,512,64]{1,2,0:T(8,128)(2,1)S(1)}, bf16[1,512,64]{1,2,0:T(8,128)(2,1)}, u32[]{:S(2)}) copy-start(bf16[1,512,64]{1,2,0:T(8,128)(2,1)} %param.23) | copy-start | bytes 196612
  56.1 99.7 %all-to-all-start.1 = ((bf16[4,768,512]{2,1,0:T(8,128)(2,1)}), bf16[4,768,512]{2,1,0:T(8,128)(2,1)}, u32[]{:S(2)}, u32[]{:S(2)}) async-start(bf16[4,768,512]{2,1,0:T(8,128)(2,1)} %bitcast.197), calls=%async_computation.1 | async-start | bytes 6291456 | tf_op jit(solution)/shard_map/all_to_all | solution.py:153
  61.4 94.5 %all-gather.4.cloned.1.call-start = ((), (), s32[]{:S(2)}) async-start(), calls=%async_computation.6 | async-start | bytes 1310720 | tf_op jit(solution)/shard_map/all_gather | solution.py:157
  199.2 72.5 %all-to-all-start.2 = ((bf16[4,768,512]{2,1,0:T(8,128)(2,1)}), bf16[4,768,512]{2,1,0:T(8,128)(2,1)}, u32[]{:S(2)}, u32[]{:S(2)}) async-start(bf16[4,768,512]{2,1,0:T(8,128)(2,1)} %get-tuple-element.150), calls=%async_computation.2 | async-start | bytes 6291456 | tf_op jit(solution)/shard_map/all_to_all | solution.py:172
  204.4 78.8 %copy-start.27 = (f32[1024]{0:T(1024)}, f32[1024]{0:T(1024)S(1)}, u32[]{:S(2)}) copy-start(f32[1024]{0:T(1024)S(1)} %fusion.74) | copy-start | bytes 12292
  204.7 78.5 %copy-start.12 = (f32[1024,2]{1,0:T(8,128)}, f32[1024,2]{1,0:T(8,128)S(1)}, u32[]{:S(2)}) copy-start(f32[1024,2]{1,0:T(8,128)S(1)} %copy.70) | copy-start | bytes 24580
  205.0 78.2 %copy-start.22 = (s32[2048]{0:T(1024)}, s32[2048]{0:T(1024)S(1)}, u32[]{:S(2)}) copy-start(s32[2048]{0:T(1024)S(1)} %broadcast_clamp_fusion) | copy-start | bytes 24580
  288.7 7.7 copy-start.6
  296.7 13.6 %copy-start.2 = (f32[1024,512]{1,0:T(8,128)}, f32[1024,512]{1,0:T(8,128)S(1)}, u32[]{:S(2)}) copy-start(f32[1024,512]{1,0:T(8,128)S(1)} %get-tuple-element.298) | copy-start | bytes 6291460
  334.3 73.8 %all-to-all-start.3 = ((bf16[4,768,512]{2,1,0:T(8,128)(2,1)}), bf16[4,768,512]{2,1,0:T(8,128)(2,1)S(1)}, u32[]{:S(2)}, u32[]{:S(2)}) async-start(bf16[4,768,512]{2,1,0:T(8,128)(2,1)} %bitcast.198), calls=%async_computation.3 | async-start | bytes 6291456 | tf_op jit(solution)/shard_map/all_to_all | solution.py:207
  338.0 190.7 %reduce-scatter.2.cloned.1.call-start = ((), (), s32[]{:S(2)}) async-start(), calls=%async_computation.7 | async-start | bytes 1310720 | tf_op jit(solution)/shard_map/reduce_scatter | solution.py:238
  478.3 135.9 %all-to-all-start.4 = ((bf16[4,768,512]{2,1,0:T(8,128)(2,1)}), bf16[4,768,512]{2,1,0:T(8,128)(2,1)S(1)}, u32[]{:S(2)}, u32[]{:S(2)}) async-start(bf16[4,768,512]{2,1,0:T(8,128)(2,1)} %get-tuple-element.155), calls=%async_computation.5 | async-start | bytes 6291456 | tf_op jit(solution)/shard_map/all_to_all | solution.py:237
  482.0 128.9 %all-reduce.5.cloned.1.call-start = ((), (), s32[]{:S(2)}) async-start(), calls=%async_computation.8 | async-start | bytes 131072 | tf_op jit(solution)/shard_map/psum | solution.py:250
  482.5 7.2 copy-start.3
  482.5 7.2 copy-start.11
  482.5 7.2 copy-start.33
  496.0 305.0 %all-reduce.7.cloned.1.call-start = ((), (), s32[]{:S(2)}) async-start(), calls=%async_computation.9 | async-start | bytes 17301504 | tf_op jit(solution)/shard_map/psum | solution.py:265
  531.2 7.2 copy-start.19
  547.3 65.2 %copy-start.14 = (bf16[1024,128]{1,0:T(8,128)(2,1)S(1)}, bf16[1024,128]{1,0:T(8,128)(2,1)}, u32[]{:S(2)}) copy-start(bf16[1024,128]{1,0:T(8,128)(2,1)} %reduce-scatter.2.cloned.1.call-done) | copy-start | bytes 786436
  547.3 65.2 %copy-start.17 = (bf16[512,128]{1,0:T(8,128)(2,1)S(1)}, bf16[512,128]{1,0:T(8,128)(2,1)}, u32[]{:S(2)}) copy-start(bf16[512,128]{1,0:T(8,128)(2,1)} %param.21) | copy-start | bytes 393220
  547.3 67.0 %copy-start.23 = (s32[2048]{0:T(1024)S(1)}, s32[2048]{0:T(1024)}, u32[]{:S(2)}) copy-start(s32[2048]{0:T(1024)} %copy-done.22) | copy-start | bytes 24580
  628.9 8.7 %copy-start.7 = (bf16[1024,512]{1,0:T(8,128)(2,1)S(1)}, bf16[1024,512]{1,0:T(8,128)(2,1)}, u32[]{:S(2)}) copy-start(bf16[1024,512]{1,0:T(8,128)(2,1)} %param.16) | copy-start | bytes 3145732
  628.9 8.7 %copy-start.21 = (f32[1024]{0:T(1024)S(1)}, f32[1024]{0:T(1024)}, u32[]{:S(2)}) copy-start(f32[1024]{0:T(1024)} %copy-done.20) | copy-start | bytes 12292
  628.9 8.7 %copy-start.25 = (f32[1024]{0:T(1024)S(1)}, f32[1024]{0:T(1024)}, u32[]{:S(2)}) copy-start(f32[1024]{0:T(1024)} %copy-done.24) | copy-start | bytes 12292
  628.9 8.7 %copy-start.31 = (f32[512]{0:T(512)S(1)}, f32[512]{0:T(512)}, u32[]{:S(2)}) copy-start(f32[512]{0:T(512)} %param.20) | copy-start | bytes 6148
  628.9 8.7 %copy-start.35 = (bf16[512,4]{0,1:T(4,128)(2,1)S(1)}, bf16[512,4]{0,1:T(4,128)(2,1)}, u32[]{:S(2)}) copy-start(bf16[512,4]{0,1:T(4,128)(2,1)} %param.22) | copy-start | bytes 12292
  637.7 45.2 %copy-start.9 = (f32[1024,512]{1,0:T(8,128)S(1)}, f32[1024,512]{1,0:T(8,128)}, u32[]{:S(2)}) copy-start(f32[1024,512]{1,0:T(8,128)} %copy-done.8) | copy-start | bytes 6291460
  (16 other events, 68.5 us)
Sparse Core Ops, SparseCore 0:
  64.3 43.4 all-gather.3
  478.4 50.2 reduce-scatter.1
  532.1 78.8 all-reduce.4
  617.5 183.4 all-reduce.6
